TPU v7x, 32 devices: a whole 2x2x4 slice. The times are simulated.
32 devices in a mesh: dp: 4 (over y, x), ctx: 8 (over z, core).
Axes of the slice: x: 2, y: 2, z: 4, core: 2. Of those that a mesh axis runs over, the one named last changes fastest.
Arguments:
- tokens: bfloat16 [4, 1024, 2048], P('dp', 'ctx'), may hold values from -6 to 6
- positions: int32 [4, 1024], P('dp', 'ctx'), may hold values from 0 to 1023, as said below
- norm_gain: float32 [2048], replicated, may hold values from 0.5 to 1.5
- norm_bias: float32 [2048], replicated, may hold values from -1.8 to 1.8
- qkv_weight: bfloat16 [2048, 6144], P('ctx'), may hold values from -0.125 to 0.125
- qkv_bias: float32 [6144], replicated, may hold values from -1.8 to 1.8
- dense_weight: bfloat16 [2048, 2048], P('ctx'), may hold values from -2 to 2
- dense_bias: float32 [2048], replicated, may hold values from -1.8 to 1.8
- up_weight: bfloat16 [2048, 8192], P('ctx'), may hold values from -0.125 to 0.125
- up_bias: float32 [8192], replicated, may hold values from -1.8 to 1.8
- down_weight: bfloat16 [8192, 2048], P('ctx'), may hold values from -0.0625 to 0.0625
- down_bias: float32 [2048], replicated, may hold values from -1.8 to 1.8
- clip_limit: int32 [32], replicated, may hold values from 3 to 11
- cotangent: bfloat16 [4, 1024, 2048], P('dp', 'ctx'), may hold values from -6 to 6
Outputs:
- layer_out: bfloat16 [4, 1024, 2048], P('dp', 'ctx')
- tokens_grad: float32 [4, 1024, 2048], P('dp', 'ctx')
- norm_gain_grad: float32 [2048], replicated
- norm_bias_grad: float32 [2048], replicated
- qkv_weight_grad: float32 [2048, 6144], P('ctx')
- qkv_bias_grad: float32 [6144], replicated
- dense_weight_grad: float32 [2048, 2048], P('ctx')
- dense_bias_grad: float32 [2048], replicated
- up_weight_grad: float32 [2048, 8192], P('ctx')
- up_bias_grad: float32 [8192], replicated
- down_weight_grad: float32 [8192, 2048], P('ctx')
- down_bias_grad: float32 [2048], replicated
- head_maxima: float32 [32], replicated
- clipped_weight: float32 [2048, 4096], P('ctx')
- clipped_bias: float32 [4096], replicated
Inputs may be any that keep to these rules, and one draw needn't show every extreme that they name: `positions`: within each sequence the ids rise by one from 0 at its first token and return to 0 at the first token of each packed document; the first sequence holds a single document.
All inputs are finite; a program needn't handle non-finite values.
Results may differ from a plain program's by a relative error of at most 0.017.
Values may be sent and summed in bfloat16 or wider, within the bound.
No kernel may reach another device: no remote copies, remote signals or barrier semaphores. Data moves between devices by JAX's collectives and lax.ppermute only.
A program may use at most 512 MiB of HBM per device.

v0:
```python
from functools import partial
import jax
import jax.numpy as jnp
from jax import lax
from jax.sharding import PartitionSpec as P

ROT = 32
EPSILON = 1e-05
MASKED = -1e30
ROPE_BASE = 10000.0
BF16 = jnp.bfloat16
F32 = jnp.float32


def rotary_tables(positions):
    half_rot = ROT // 2
    frequency = ROPE_BASE ** (-(jnp.arange(half_rot, dtype=F32) * 2.0 / ROT))
    angles = positions.astype(F32)[..., None] * frequency
    cosine = jnp.cos(angles)
    sine = jnp.sin(angles)
    return (
        jnp.concatenate([cosine, cosine], -1)[..., None, :],
        jnp.concatenate([sine, sine], -1)[..., None, :],
    )


def rotate(values, cosine, sine):
    half_rot = ROT // 2
    turned = values[..., :ROT]
    swapped = jnp.concatenate([-turned[..., half_rot:], turned[..., :half_rot]], -1)
    return jnp.concatenate([turned * cosine + swapped * sine, values[..., ROT:]], -1)


def rotate_back(gradient, cosine, sine):
    half_rot = ROT // 2
    turned = gradient[..., :ROT]
    scaled = turned * sine
    swapped = jnp.concatenate([scaled[..., half_rot:], -scaled[..., :half_rot]], -1)
    return jnp.concatenate([turned * cosine + swapped, gradient[..., ROT:]], -1)


def dot(left, right, contract):
    return lax.dot_general(
        left, right, ((contract[:1], contract[1:]), ((), ())), preferred_element_type=F32
    )


def per_device(
    tokens,
    positions,
    norm_gain,
    norm_bias,
    qkv_weight,
    qkv_bias,
    dense_weight,
    dense_bias,
    up_weight,
    up_bias,
    down_weight,
    down_bias,
    clip_limit,
    cotangent,
):
    seqs, stretch, width = tokens.shape
    heads = clip_limit.shape[0]
    head_dim = width // heads
    rows = seqs * stretch
    parts = lax.axis_size("ctx")
    part = lax.axis_index("ctx")
    own_heads = heads // parts
    own = own_heads * head_dim
    own_rows = qkv_weight.shape[0]
    own_ff = down_weight.shape[0]
    length = stretch * parts
    all_rows = seqs * length
    scale = head_dim ** (-0.5)
    pieces = jnp.concatenate(
        [
            qkv_weight.reshape(own_rows, 3, parts, own)
            .transpose(2, 0, 1, 3)
            .reshape(parts, own_rows, 3 * own),
            up_weight.reshape(own_rows, parts, own_ff).transpose(1, 0, 2),
        ],
        axis=2,
    )
    in_weight = lax.all_to_all(pieces, "ctx", split_axis=0, concat_axis=0, tiled=True).reshape(
        width, 3 * own + own_ff
    )
    grad_rows = lax.all_gather(cotangent, "ctx", axis=1, tiled=True).reshape(all_rows, width)
    inputs = tokens.reshape(rows, width).astype(F32)
    centre = inputs - jnp.mean(inputs, axis=-1, keepdims=True)
    inv_std = lax.rsqrt(jnp.mean(centre * centre, axis=-1, keepdims=True) + EPSILON)
    normed = centre * inv_std
    hidden_local = (normed * norm_gain + norm_bias).astype(BF16)
    hidden = lax.all_gather(
        hidden_local.reshape(seqs, stretch, width), "ctx", axis=1, tiled=True
    ).reshape(all_rows, width)
    all_positions = lax.all_gather(positions, "ctx", axis=1, tiled=True)
    qkv_own_bias = lax.dynamic_slice_in_dim(
        qkv_bias.reshape(3, parts, own), part, 1, axis=1
    ).reshape(3 * own)
    up_own_bias = lax.dynamic_slice_in_dim(up_bias, part * own_ff, own_ff)
    projected = dot(hidden, in_weight, (1, 0))
    joined = projected[:, : 3 * own] + qkv_own_bias
    upward = projected[:, 3 * own :] + up_own_bias
    cosine, sine = rotary_tables(all_positions)
    shaped = joined.reshape(seqs, length, 3, own_heads, head_dim)
    queries = rotate(shaped[:, :, 0], cosine, sine).astype(BF16)
    keys = rotate(shaped[:, :, 1], cosine, sine).astype(BF16)
    values = shaped[:, :, 2].astype(BF16)
    place = jnp.arange(length, dtype=jnp.int32)
    allowed = place[:, None] >= place[None, :]
    scores = jnp.einsum("sqhd,skhd->shqk", queries, keys, preferred_element_type=F32) * scale
    scores = jnp.where(allowed, scores, MASKED)
    row_max = jnp.max(scores, axis=-1, keepdims=True)
    expo = jnp.exp(scores - row_max)
    row_sum = jnp.sum(expo, axis=-1, keepdims=True)
    probs = expo / row_sum
    probs_low = probs.astype(BF16)
    mixed = jnp.einsum("shqk,skhd->sqhd", probs_low, values, preferred_element_type=F32)
    attended = mixed.reshape(all_rows, own).astype(BF16)
    own_maxima = jnp.max(row_max, axis=(0, 2, 3))
    slots = lax.dynamic_update_slice_in_dim(
        jnp.full((heads,), MASKED, F32), own_maxima, part * own_heads, axis=0
    )
    head_maxima = lax.pmax(slots, ("dp", "ctx"))
    activated = jax.nn.gelu(upward, approximate=True).astype(BF16)
    branch = dot(attended, dense_weight, (1, 0)) + dot(activated, down_weight, (1, 0))
    branch_sum = lax.psum_scatter(
        branch.astype(BF16).reshape(seqs, length, width), "ctx", scatter_dimension=1, tiled=True
    ).reshape(rows, width)
    layer_out = (inputs + branch_sum.astype(F32) + dense_bias + down_bias).astype(BF16)
    mixed_grad = dot(grad_rows, dense_weight, (1, 1)).astype(BF16)
    act_grad = dot(grad_rows, down_weight, (1, 1))
    dense_grad = dot(attended, grad_rows, (0, 0))
    down_grad = dot(activated, grad_rows, (0, 0))
    out_bias_grad = jnp.sum(cotangent.reshape(rows, width).astype(F32), axis=0)
    unused_value, gelu_back = jax.vjp(partial(jax.nn.gelu, approximate=True), upward)
    up_low = gelu_back(act_grad)[0].astype(BF16)
    mixed_low = mixed_grad.reshape(seqs, length, own_heads, head_dim)
    value_grad = jnp.einsum("shqk,sqhd->skhd", probs_low, mixed_low, preferred_element_type=F32)
    prob_grad = jnp.einsum("sqhd,skhd->shqk", mixed_low, values, preferred_element_type=F32)
    delta = jnp.sum(probs * prob_grad, axis=-1, keepdims=True)
    score_grad = (probs * (prob_grad - delta)).astype(BF16)
    query_grad = jnp.einsum("shqk,skhd->sqhd", score_grad, keys, preferred_element_type=F32) * scale
    key_grad = (
        jnp.einsum("shqk,sqhd->skhd", score_grad, queries, preferred_element_type=F32) * scale
    )
    joined_low = (
        jnp.stack(
            [
                rotate_back(query_grad, cosine, sine),
                rotate_back(key_grad, cosine, sine),
                value_grad,
            ],
            axis=2,
        )
        .reshape(all_rows, 3 * own)
        .astype(BF16)
    )
    both = jnp.concatenate([joined_low, up_low], axis=1)
    hidden_part = dot(both, in_weight, (1, 1))
    hidden_grad = (
        lax.psum_scatter(
            hidden_part.astype(BF16).reshape(seqs, length, width),
            "ctx",
            scatter_dimension=1,
            tiled=True,
        )
        .reshape(rows, width)
        .astype(F32)
    )
    in_grad = dot(hidden, both, (0, 0)).astype(BF16)
    in_quarter = lax.psum_scatter(
        in_grad.reshape(parts, own_rows, 3 * own + own_ff), "dp", scatter_dimension=1, tiled=True
    )
    in_quarter = lax.all_to_all(in_quarter, "ctx", split_axis=0, concat_axis=0, tiled=True)
    in_rows = lax.all_gather(in_quarter.transpose(1, 0, 2), "dp", axis=0, tiled=True)
    qkv_grad = (
        in_rows[:, :, : 3 * own]
        .reshape(own_rows, parts, 3, own)
        .transpose(0, 2, 1, 3)
        .reshape(own_rows, 3 * width)
        .astype(F32)
    )
    up_grad = in_rows[:, :, 3 * own :].reshape(own_rows, parts * own_ff).astype(F32)
    out_grad = lax.psum(jnp.concatenate([dense_grad, down_grad], axis=0).astype(BF16), "dp")
    gain_part = jnp.sum(hidden_grad * normed, axis=0)
    shift_part = jnp.sum(hidden_grad, axis=0)
    scaled = hidden_grad * norm_gain
    tokens_grad = cotangent.reshape(rows, width).astype(F32) + inv_std * (
        scaled
        - jnp.mean(scaled, axis=-1, keepdims=True)
        - normed * jnp.mean(scaled * normed, axis=-1, keepdims=True)
    )
    qkv_bias_part = lax.dynamic_update_slice(
        jnp.zeros((3, parts, own), F32),
        jnp.sum(joined_low.astype(F32), axis=0).reshape(3, 1, own),
        (0, part, 0),
    ).reshape(3 * width)
    up_bias_part = lax.dynamic_update_slice(
        jnp.zeros((parts * own_ff,), F32), jnp.sum(up_low.astype(F32), axis=0), (part * own_ff,)
    )
    gain_grad, shift_grad, qkv_bias_grad, out_bias_grad, up_bias_grad = lax.psum(
        (gain_part, shift_part, qkv_bias_part, out_bias_grad, up_bias_part), ("dp", "ctx")
    )
    limits = clip_limit.astype(F32)
    factor = limits / jnp.maximum(head_maxima, limits)
    column_scale = jnp.tile(jnp.repeat(jnp.sqrt(factor), head_dim), 2)
    clipped_weight = qkv_weight[:, : 2 * width].astype(F32) * column_scale
    clipped_bias = qkv_bias[: 2 * width] * column_scale
    return (
        layer_out.reshape(seqs, stretch, width),
        tokens_grad.reshape(seqs, stretch, width),
        gain_grad,
        shift_grad,
        qkv_grad,
        qkv_bias_grad,
        out_grad[:own].astype(F32),
        out_bias_grad,
        up_grad,
        up_bias_grad,
        out_grad[own:].astype(F32),
        out_bias_grad,
        head_maxima,
        clipped_weight,
        clipped_bias,
    )


def solution(mesh):
    rows = P("dp", "ctx", None)
    weight = P("ctx", None)
    in_specs = (rows, P("dp", "ctx"), P(), P()) + (weight, P()) * 4 + (P(), rows)
    out_specs = (rows, rows, P(), P()) + (weight, P()) * 4 + (P(), weight, P())
    return jax.shard_map(
        per_device, mesh=mesh, in_specs=in_specs, out_specs=out_specs, check_vma=False
    )
```

profile of v0, /device:TPU:0, one launch (start us, length us, event | category | flops | bytes accessed | tf_op | source)
XLA Modules:
  0.0 971.7 jit_solution(4422547686251745322)
XLA Ops:
  7.9 4.6 copy.74
  12.6 3.9 copy.75
  16.4 6.4 copy.76
  22.9 6.7 pad_maximum_fusion
  29.6 6.5 all-to-all-start
  38.6 174.2 %all_gather.13 = s32[1,1024]{1,0:T(1,128)S(1)} all-gather(s32[1,128]{1,0:T(1,128)S(1)} %copy-done.37), channel_id=1, replica_groups=mesh['dp'=4,'ctx'=8] {'ctx'}, dimensions={1}, use_global_device_ids=true | all-gather | bytes 4608 | tf_op jit(solution)/shard_map/all_gather | solution.py:98
  214.9 4.6 fusion.47
  219.5 29.4 %all-to-all-done = bf16[8,256,1792]{1,2,0:T(8,128)(2,1)} async-done(((bf16[8,256,1792]{1,2,0:T(8,128)(2,1)}), bf16[8,256,1792]{1,2,0:T(8,128)(2,1)}, u32[]{:S(2)}, u32[]{:S(2)}) %all-to-all-start) | async-done | bytes 7340064 | tf_op jit(solution)/shard_map/all_to_all | solution.py:86
  248.9 9.9 %copy.77 = bf16[8,256,1792]{2,1,0:T(8,128)(2,1)} copy(bf16[8,256,1792]{1,2,0:T(8,128)(2,1)} %all-to-all-done) | data formatting | bytes 14680064 | tf_op jit(solution)/shard_map/all_to_all | solution.py:86
  258.9 11.6 %fusion.22 = f32[1024,1792]{1,0:T(8,128)S(1)} fusion(bf16[2048,1792]{1,0:T(8,128)(2,1)} %bitcast.151, bf16[1,1024,2048]{2,1,0:T(8,128)(2,1)} %all-gather.4.cloned.1.call-done), kind=kOutput, calls=%fused_computation.37 | convolution fusion | flops 7516192768 | bytes 18874368 | tf_op jit(solution)/shard_map/dot_general | solution.py:43
  270.5 3.0 copy-done.5
  275.5 3.5 copy.78
  281.1 10.4 %fusion.95 = (f32[4,1024]{1,0:T(4,128)S(1)}, f32[4,1024,1024]{1,2,0:T(8,128)}) fusion(pred[1024,1024]{0,1:T(8,128)(4,1)S(1)} %iota_compare_fusion, bf16[1024,4,32]{0,2,1:T(8,128)(2,1)S(1)} %get-tuple-element.118, bf16[1024,4,32]{0,2,1:T(8,128)(2,1)S(1)} %get-tuple-element.104, bf16[1024,4,32]{0,2,1:T(8,128)(2,1)S(1)} %get-tuple-element.117, ...), kind=kOutput, calls=%fused_computation.150 | convolution fusion | flops 555746304 | bytes 18890752 | tf_op jit(solution)/shard_map/sub | solution.py:116
  291.6 9.6 fusion.37
  301.2 15.9 %multiply_reduce_fusion = (f32[4,1024]{1,0:T(4,128)S(1)}, f32[4,1024,1024]{1,2,0:T(8,128)}) fusion(f32[4,1024,1024]{1,2,0:T(8,128)} %get-tuple-element.112, f32[4,1024]{1,0:T(4,128)S(1)} %get-tuple-element.111, bf16[1024,4,64]{0,2,1:T(8,128)(2,1)} %bitcast.164, f32[1,1024,3,4,64]{1,4,3,2,0:T(8,128)} %bitcast.148), kind=kOutput, calls=%fused_computation.2 | convolution fusion | flops 549449728 | bytes 34635776 | tf_op jit(solution)/shard_map/sqhd,skhd->shqk/dot_general | solution.py:142
  317.1 8.0 multiply_convert_fusion
  325.2 2.7 fusion.40
  332.5 12.3 %convert_reduce_fusion = (f32[1024]{0:T(1024)}, bf16[1024,1024]{1,0:T(8,128)(2,1)S(1)}) fusion(f32[1024]{0:T(1024)S(1)} %copy-done.35, f32[1024,1792]{1,0:T(8,128)} %copy-done.5, bf16[1024,2048]{1,0:T(8,128)(2,1)} %param.24, bf16[1,1024,2048]{2,1,0:T(8,128)(2,1)} %all-gather.6.cloned.1.call-done), kind=kOutput, calls=%fused_computation.40 | convolution fusion | flops 4319083520 | bytes 14688256 | tf_op jit(solution)/shard_map/dot_general | solution.py:43
  344.8 8.5 convolution_convert_fusion
  353.3 7.0 copy.84
  360.4 12.0 %convert_bitcast_fusion.1 = bf16[1,1024,2048]{2,1,0:T(8,128)(2,1)} fusion(bf16[2048,1792]{1,0:T(8,128)(2,1)} %bitcast.152, bf16[1024,1024]{1,0:T(8,128)(2,1)} %copy-done.42, bf16[1024,768]{1,0:T(8,128)(2,1)S(1)} %copy-done.4), kind=kOutput, calls=%fused_computation.41 | convolution fusion | flops 7525629952 | bytes 15204352 | tf_op jit(solution)/shard_map/dot_general | solution.py:43
  373.4 9.1 fusion.44
  382.5 8.5 fusion.92
  391.0 3.3 fusion.31
  394.6 3.6 fusion.34
  398.2 8.8 fusion.28
  407.0 2.8 pad_maximum_fusion.1
  409.9 38.0 %reduce-scatter.8.cloned.1.call-done = bf16[8,64,1792]{2,0,1:T(8,128)(2,1)} async-done(((bf16[8,256,1792]{2,0,1:T(8,128)(2,1)}), bf16[8,64,1792]{2,0,1:T(8,128)(2,1)}) %reduce-scatter.8.cloned.1.call-update) | async-done | bytes 1835024 | tf_op jit(solution)/shard_map/reduce_scatter | solution.py:174
  448.0 3.0 copy.85
  451.0 4.6 all-to-all-start.1
  456.7 78.3 %reduce-scatter.6.cloned.1.call-done = bf16[1,128,2048]{2,1,0:T(8,128)(2,1)} async-done(((bf16[1,1024,2048]{2,1,0:T(8,128)(2,1)}), bf16[1,128,2048]{2,1,0:T(8,128)(2,1)}) %reduce-scatter.6.cloned.1.call-update) | async-done | bytes 524304 | tf_op jit(solution)/shard_map/reduce_scatter | solution.py:164
  537.1 53.5 %reduce-scatter.4.cloned.1.call-done = bf16[1,128,2048]{2,1,0:T(8,128)(2,1)} async-done(((bf16[1,1024,2048]{2,1,0:T(8,128)(2,1)}), bf16[1,128,2048]{2,1,0:T(8,128)(2,1)}) %reduce-scatter.4.cloned.1.call-update) | async-done | bytes 524304 | tf_op jit(solution)/shard_map/reduce_scatter | solution.py:129
  590.7 3.9 convert_reduce_fusion.4
  594.7 2.2 copy.86
  597.0 5.4 fusion.1
  602.5 38.0 %pmax.7 = f32[32]{0:T(128)S(1)} all-reduce(f32[32]{0:T(128)S(1)} %dynamic_update_slice.11), channel_id=1, replica_groups=mesh['dp'=4,'ctx'=8] {'dp','ctx'}, use_global_device_ids=true, to_apply=%region_22.23 | all-reduce | flops 32 | bytes 256 | tf_op jit(solution)/shard_map/pmax | solution.py:126
  641.3 4.1 convert_multiply_fusion
  645.5 69.2 %all-reduce.4.cloned.1.call-done = bf16[1280,2048]{1,0:T(8,128)(2,1)} async-done(((bf16[1280,2048]{1,0:T(8,128)(2,1)}), bf16[1280,2048]{1,0:T(8,128)(2,1)}) %all-reduce.4.cloned.1.call-update) | async-done | bytes 5242896 | tf_op jit(solution)/shard_map/psum | solution.py:187
  714.7 2.8 slice_convert_fusion.2
  717.5 6.7 slice_convert_fusion
  724.1 120.5 %all-reduce.6.cloned.1.call-done = (f32[2048]{0:T(1024)}, f32[2048]{0:T(1024)}, f32[6144]{0:T(1024)}, f32[2048]{0:T(1024)}, f32[8192]{0:T(1024)}) async-done(((f32[2048]{0:T(1024)}, f32[2048]{0:T(1024)}, f32[6144]{0:T(1024)}, f32[2048]{0:T(1024)}, f32[8192]{0:T(1024)}), (f32[2048]{0:T(1024)}, f32[2048]{0:T(1024)}, f32[6144]{0:T(1024)}, f32[2048]{0:T(1024)}, f32[8192]{0:T(1024)})) %all-reduce.6.cloned.1.call-update) | async-done | bytes 81936 | tf_op jit(solution)/shard_map/psum | solution.py:204
  844.6 82.7 %all-gather.8.cloned.1.call-done = bf16[256,8,1792]{2,1,0:T(8,128)(2,1)} async-done(((bf16[64,8,1792]{2,1,0:T(8,128)(2,1)}), bf16[256,8,1792]{2,1,0:T(8,128)(2,1)}) %all-gather.8.cloned.1.call-update) | async-done | bytes 7340048 | tf_op jit(solution)/shard_map/all_gather | solution.py:178
  927.3 3.8 slice.136
  931.1 5.0 copy.94
  936.1 3.2 slice_convert_fusion.1
  939.3 11.0 %copy.96 = f32[32,8,8,1024]{3,1,2,0:T(8,128)} copy(f32[32,8,8,1024]{3,2,1,0:T(8,128)S(1)} %bitcast.139) | data formatting | bytes 16777216
  951.1 3.3 copy.88
  954.4 6.6 copy.89
  (165 shorter events, 23.6 us)
Async XLA Ops:
  7.2 207.7 %copy-start = (bf16[256,2048]{1,0:T(8,128)(2,1)S(1)}, bf16[256,2048]{1,0:T(8,128)(2,1)}, u32[]{:S(2)}) copy-start(bf16[256,2048]{1,0:T(8,128)(2,1)} %param.20) | copy-start | bytes 3145732
  7.2 207.7 %all-gather.6.cloned.1.call-start = ((), (), s32[]{:S(2)}) async-start(), calls=%async_computation.7 | async-start | bytes 4718592 | tf_op jit(solution)/shard_map/all_gather | solution.py:89
  29.6 6.6 copy-start.1
  29.6 7.8 copy-start.19
  29.6 7.8 copy-start.28
  29.6 9.1 copy-start.37
  29.6 183.3 %copy-start.21 = (f32[6144]{0:T(1024)S(1)}, f32[6144]{0:T(1024)}, u32[]{:S(2)}) copy-start(f32[6144]{0:T(1024)} %param.19) | copy-start | bytes 73732
  29.6 219.4 %all-to-all-start = ((bf16[8,256,1792]{1,2,0:T(8,128)(2,1)}), bf16[8,256,1792]{1,2,0:T(8,128)(2,1)}, u32[]{:S(2)}, u32[]{:S(2)}) async-start(bf16[8,256,1792]{1,2,0:T(8,128)(2,1)} %pad_maximum_fusion), calls=%async_computation | async-start | bytes 14680064 | tf_op jit(solution)/shard_map/all_to_all | solution.py:86
  36.1 222.8 %all-gather.4.cloned.1.call-start = ((), (), s32[]{:S(2)}) async-start(), calls=%async_computation.5 | async-start | bytes 4718592 | tf_op jit(solution)/shard_map/all_gather | solution.py:95
  38.6 409.4 %reduce-scatter.8.cloned.1.call-start = ((), (), s32[]{:S(2)}) async-start(), calls=%async_computation.9 | async-start | bytes 9175040 | tf_op jit(solution)/shard_map/reduce_scatter | solution.py:174
  214.9 76.7 %copy-start.6 = (pred[1024,1024]{0,1:T(8,128)(4,1)}, pred[1024,1024]{0,1:T(8,128)(4,1)S(1)}, u32[]{:S(2)}) copy-start(pred[1024,1024]{0,1:T(8,128)(4,1)S(1)} %iota_compare_fusion) | copy-start | bytes 3145732
  270.5 3.1 copy-start.5
  280.7 10.8 %copy-start.9 = (bf16[1024,4,32]{0,2,1:T(8,128)(2,1)}, bf16[1024,4,32]{0,2,1:T(8,128)(2,1)S(1)}, u32[]{:S(2)}) copy-start(bf16[1024,4,32]{0,2,1:T(8,128)(2,1)S(1)} %get-tuple-element.118) | copy-start | bytes 786436
  280.8 92.2 %copy-start.7 = (bf16[1024,4,32]{0,2,1:T(8,128)(2,1)}, bf16[1024,4,32]{0,2,1:T(8,128)(2,1)S(1)}, u32[]{:S(2)}) copy-start(bf16[1024,4,32]{0,2,1:T(8,128)(2,1)S(1)} %get-tuple-element.117) | copy-start | bytes 786436
  281.1 10.5 %copy-start.12 = (bf16[1024,4,32]{0,2,1:T(8,128)(2,1)}, bf16[1024,4,32]{0,2,1:T(8,128)(2,1)S(1)}, u32[]{:S(2)}) copy-start(bf16[1024,4,32]{0,2,1:T(8,128)(2,1)S(1)} %get-tuple-element.103) | copy-start | bytes 786436
  281.1 10.5 %copy-start.14 = (bf16[1024,4,32]{0,2,1:T(8,128)(2,1)}, bf16[1024,4,32]{0,2,1:T(8,128)(2,1)S(1)}, u32[]{:S(2)}) copy-start(bf16[1024,4,32]{0,2,1:T(8,128)(2,1)S(1)} %get-tuple-element.104) | copy-start | bytes 786436
  301.2 15.9 %slice-start = ((s8[16777216]{0:T(1024)(128)(4,1)}), s8[4194304]{0:T(1024)(128)(4,1)S(1)}, s32[]{:S(2)}) async-start(s8[16777216]{0:T(1024)(128)(4,1)} %bitcast.142), calls=%async_computation.13 | async-start | bytes 8388608
  301.2 15.9 %slice-start.1 = ((s8[16777216]{0:T(1024)(128)(4,1)}), s8[4194304]{0:T(1024)(128)(4,1)S(1)}, s32[]{:S(2)}) async-start(s8[16777216]{0:T(1024)(128)(4,1)} %bitcast.142), calls=%async_computation.14 | async-start | bytes 8388608
  301.2 15.9 %slice-start.2 = ((s8[16777216]{0:T(1024)(128)(4,1)}), s8[4194304]{0:T(1024)(128)(4,1)S(1)}, s32[]{:S(2)}) async-start(s8[16777216]{0:T(1024)(128)(4,1)} %bitcast.142), calls=%async_computation.15 | async-start | bytes 8388608
  301.2 15.9 %slice-start.3 = ((s8[16777216]{0:T(1024)(128)(4,1)}), s8[4194304]{0:T(1024)(128)(4,1)S(1)}, s32[]{:S(2)}) async-start(s8[16777216]{0:T(1024)(128)(4,1)} %bitcast.142), calls=%async_computation.16 | async-start | bytes 8388608
  317.1 8.1 copy-start.13
  332.5 12.3 %copy-start.4 = (bf16[1024,768]{1,0:T(8,128)(2,1)S(1)}, bf16[1024,768]{1,0:T(8,128)(2,1)}, u32[]{:S(2)}) copy-start(bf16[1024,768]{1,0:T(8,128)(2,1)} %copy.83) | copy-start | bytes 4718596
  332.5 12.3 %copy-start.39 = (bf16[1,1024,2048]{2,1,0:T(8,128)(2,1)S(1)}, bf16[1,1024,2048]{2,1,0:T(8,128)(2,1)}, u32[]{:S(2)}) copy-start(bf16[1,1024,2048]{2,1,0:T(8,128)(2,1)} %all-gather.4.cloned.1.call-done) | copy-start | bytes 12582916
  344.8 8.5 copy-start.42
  360.3 174.7 %reduce-scatter.6.cloned.1.call-start = ((), (), s32[]{:S(2)}) async-start(), calls=%async_computation.8 | async-start | bytes 4718592 | tf_op jit(solution)/shard_map/reduce_scatter | solution.py:164
  372.4 218.2 %reduce-scatter.4.cloned.1.call-start = ((), (), s32[]{:S(2)}) async-start(), calls=%async_computation.6 | async-start | bytes 4718592 | tf_op jit(solution)/shard_map/reduce_scatter | solution.py:129
  394.4 320.3 %all-reduce.4.cloned.1.call-start = ((), (), s32[]{:S(2)}) async-start(), calls=%async_computation.11 | async-start | bytes 10485760 | tf_op jit(solution)/shard_map/psum | solution.py:187
  394.6 3.6 copy-start.38
  409.9 46.6 %copy-start.36 = (f32[1024]{0:T(1024)S(1)}, f32[1024]{0:T(1024)}, u32[]{:S(2)}) copy-start(f32[1024]{0:T(1024)} %get-tuple-element.115) | copy-start | bytes 12292
  409.9 125.1 %copy-start.2 = (bf16[1,128,2048]{2,1,0:T(8,128)(2,1)S(1)}, bf16[1,128,2048]{2,1,0:T(8,128)(2,1)}, u32[]{:S(2)}) copy-start(bf16[1,128,2048]{2,1,0:T(8,128)(2,1)} %param.14) | copy-start | bytes 1572868
  409.9 125.1 %copy-start.20 = (f32[2048]{0:T(1024)S(1)}, f32[2048]{0:T(1024)}, u32[]{:S(2)}) copy-start(f32[2048]{0:T(1024)} %param.16) | copy-start | bytes 24580
  409.9 125.1 %copy-start.27 = (f32[128]{0:T(128)S(1)}, f32[128]{0:T(128)}, u32[]{:S(2)}) copy-start(f32[128]{0:T(128)} %copy-done.26) | copy-start | bytes 1540
  409.9 125.1 %copy-start.34 = (f32[128]{0:T(128)S(1)}, f32[128]{0:T(128)}, u32[]{:S(2)}) copy-start(f32[128]{0:T(128)} %copy-done.33) | copy-start | bytes 1540
  409.9 180.8 %copy-start.29 = (f32[2048]{0:T(1024)S(1)}, f32[2048]{0:T(1024)}, u32[]{:S(2)}) copy-start(f32[2048]{0:T(1024)} %param.25) | copy-start | bytes 24580
  409.9 180.7 %copy-start.30 = (f32[2048]{0:T(1024)S(1)}, f32[2048]{0:T(1024)}, u32[]{:S(2)}) copy-start(f32[2048]{0:T(1024)} %param.21) | copy-start | bytes 24580
  451.0 143.6 %all-to-all-start.1 = ((bf16[8,64,1792]{2,1,0:T(8,128)(2,1)}), bf16[8,64,1792]{2,1,0:T(8,128)(2,1)S(1)}, u32[]{:S(2)}, u32[]{:S(2)}) async-start(bf16[8,64,1792]{2,1,0:T(8,128)(2,1)} %copy.85), calls=%async_computation.4 | async-start | bytes 3670016 | tf_op jit(solution)/shard_map/all_to_all | solution.py:177
  455.6 389.0 %all-reduce.6.cloned.1.call-start = ((), (), s32[]{:S(2)}) async-start(), calls=%async_computation.12 | async-start | bytes 163840 | tf_op jit(solution)/shard_map/psum | solution.py:204
  456.7 137.9 %copy-start.18 = (f32[8192]{0:T(1024)}, f32[8192]{0:T(1024)S(1)}, u32[]{:S(2)}) copy-start(f32[8192]{0:T(1024)S(1)} %dynamic_update_slice.10) | copy-start | bytes 98308
  594.6 332.7 %all-gather.8.cloned.1.call-start = ((), (), s32[]{:S(2)}) async-start(), calls=%async_computation.10 | async-start | bytes 9175040 | tf_op jit(solution)/shard_map/all_gather | solution.py:178
  597.0 43.6 %copy-start.40 = (s32[32]{0:T(128)S(1)}, s32[32]{0:T(128)}, u32[]{:S(2)}) copy-start(s32[32]{0:T(128)} %param.26) | copy-start | bytes 388
  597.0 43.7 %copy-start.22 = (f32[6144]{0:T(1024)S(1)}, f32[6144]{0:T(1024)}, u32[]{:S(2)}) copy-start(f32[6144]{0:T(1024)} %param.19) | copy-start | bytes 73732
  640.5 76.9 %copy-start.41 = (f32[32]{0:T(128)}, f32[32]{0:T(128)S(1)}, u32[]{:S(2)}) copy-start(f32[32]{0:T(128)S(1)} %pmax.7) | copy-start | bytes 388
  939.3 11.0 %copy-start.3 = (bf16[256,8,768]{0,2,1:T(8,128)(2,1)S(1)}, bf16[256,8,768]{0,2,1:T(8,128)(2,1)}, u32[]{:S(2)}) copy-start(bf16[256,8,768]{0,2,1:T(8,128)(2,1)} %copy.94) | copy-start | bytes 9437188
  954.4 6.6 copy-start.24
  954.4 7.2 copy-start.32
  954.4 7.8 copy-start.31
  954.4 8.4 copy-start.25
  954.4 9.6 copy-start.23
  (9 other events, 15.6 us)
Sparse Core Ops, SparseCore 0:
  9.6 67.6 all-gather.5
  79.5 135.0 all-gather.3
  360.5 87.4 reduce-scatter.7
  450.7 84.2 reduce-scatter.5
  537.7 52.9 reduce-scatter.3
  594.4 120.2 all-reduce.3
  722.2 122.3 all-reduce.5
  847.1 80.2 all-gather.7
where the time goes:
time: 976 us; the launch traced here: 972 us
  waiting for transfers between devices  473 us (48%)
  blocking collectives  212 us (22%)
  matrix products  128 us (13%)
  local copies, waits for them, and re-layouts  84.9 us (9%)
  other arithmetic  47 us (5%)
  between operations  15 us (2%)
  starting transfers between devices  12 us (1%)
    all_gather x1, blocking collectives, per_device(): all_positions = lax.all_gather(positions, 'ctx', axis=1, tiled=True)  174 us
    psum x1, waiting for transfers between devices, per_device(): lax.psum((gain_part, shift_part, qkv_bias_part, out_bias_grad, up_bias_pa...  121 us
    all_gather x1, waiting for transfers between devices, per_device(): lax.all_gather(in_quarter.transpose(1, 0, 2), 'dp', axis=0, tiled=True)  82.7 us
    reduce_scatter x1, waiting for transfers between devices, per_device(): lax.psum_scatter(hidden_part.astype(BF16).reshape(seqs, length, width), '...  78.3 us
    dot_general x9, matrix products, dot(): lax.dot_general(left, right, ((contract[:1], contract[1:]), ((), ())), pr...  73.4 us
    psum x1, waiting for transfers between devices, per_device(): lax.psum(jnp.concatenate([dense_grad, down_grad], axis=0).astype(BF16), '...  69.2 us
    reduce_scatter x1, waiting for transfers between devices, per_device(): lax.psum_scatter(branch.astype(BF16).reshape(seqs, length, width), 'ctx',...  53.5 us
    unnamed x108, local copies, waits for them, and re-layouts  42.9 us
  transfers between devices with their start and end apart: 10, of which 7 were waited for; matrix products, arithmetic and copies ran while one was open for 12% of the time, Pallas kernels for 0%

commit v1 on v0

--- a/solution.py
+++ b/solution.py
@@ -184,7 +184,9 @@
         .astype(F32)
     )
     up_grad = in_rows[:, :, 3 * own :].reshape(own_rows, parts * own_ff).astype(F32)
-    out_grad = lax.psum(jnp.concatenate([dense_grad, down_grad], axis=0).astype(BF16), "dp")
+    out_grad = jnp.sum(
+        lax.all_gather(jnp.concatenate([dense_grad, down_grad], axis=0).astype(BF16), "dp"), axis=0
+    )
     gain_part = jnp.sum(hidden_grad * normed, axis=0)
     shift_part = jnp.sum(hidden_grad, axis=0)
     scaled = hidden_grad * norm_gain

time: 976 us -> 1040 us (1.066)
  waiting for transfers between devices: 473 us -> 517 us
  other arithmetic: 47 us -> 63.1 us
    all_gather x0 -> x1, waiting for transfers between devices: none -> 160 us  [per_device(): lax.all_gather(jnp.concatenate([dense_grad, down_grad], axis=0).astype(BF...]
    psum x1 -> x0, waiting for transfers between devices: 69.2 us -> none  [per_device(): lax.psum(jnp.concatenate([dense_grad, down_grad], axis=0).astype(BF16), '...]
    psum x1, waiting for transfers between devices: 121 us -> 58.9 us  [per_device(): lax.psum((gain_part, shift_part, qkv_bias_part, out_bias_grad, up_bias_pa...]
    reduce_scatter x1, waiting for transfers between devices: 38 us -> 53.3 us  [per_device(): lax.psum_scatter(in_grad.reshape(parts, own_rows, 3 * own + own_ff), 'dp'...]
    reduce_sum x0 -> x1, other arithmetic: none -> 14.8 us  [per_device(): jnp.sum(lax.all_gather(jnp.concatenate([dense_grad, down_grad], axis=0).a...]
    unnamed x108 -> x120, local copies, waits for them, and re-layouts: 42.9 us -> 44.7 us
  transfers between devices with their start and end apart: 10 -> 10, of which waited for: 7 -> 7; matrix products, arithmetic and copies ran while one was open for 12% -> 14% of each run, Pallas kernels for 0% -> 0%
where the time goes in v1:
time: 1040 us; the launch traced here: 1030 us
  waiting for transfers between devices  517 us (50%)
  blocking collectives  212 us (20%)
  matrix products  126 us (12%)
  local copies, waits for them, and re-layouts  86.9 us (8%)
  other arithmetic  63.1 us (6%)
  between operations  15.3 us (1%)
  starting transfers between devices  11.6 us (1%)
    all_gather x1, blocking collectives, per_device(): all_positions = lax.all_gather(positions, 'ctx', axis=1, tiled=True)  174 us
    all_gather x1, waiting for transfers between devices, per_device(): lax.all_gather(jnp.concatenate([dense_grad, down_grad], axis=0).astype(BF...  160 us
    all_gather x1, waiting for transfers between devices, per_device(): lax.all_gather(in_quarter.transpose(1, 0, 2), 'dp', axis=0, tiled=True)  82.7 us
    reduce_scatter x1, waiting for transfers between devices, per_device(): lax.psum_scatter(hidden_part.astype(BF16).reshape(seqs, length, width), '...  78.1 us
    dot_general x9, matrix products, dot(): lax.dot_general(left, right, ((contract[:1], contract[1:]), ((), ())), pr...  73.3 us
    psum x1, waiting for transfers between devices, per_device(): lax.psum((gain_part, shift_part, qkv_bias_part, out_bias_grad, up_bias_pa...  58.9 us
    reduce_scatter x1, waiting for transfers between devices, per_device(): lax.psum_scatter(branch.astype(BF16).reshape(seqs, length, width), 'ctx',...  53.4 us
    reduce_scatter x1, waiting for transfers between devices, per_device(): lax.psum_scatter(in_grad.reshape(parts, own_rows, 3 * own + own_ff), 'dp'...  53.3 us
  transfers between devices with their start and end apart: 10, of which 7 were waited for; matrix products, arithmetic and copies ran while one was open for 14% of the time, Pallas kernels for 0%

profile of v1, /device:TPU:0, one launch (start us, length us, event | category | flops | bytes accessed | tf_op | source)
XLA Modules:
  0.0 1031.6 jit_solution(18341694140487957121)
XLA Ops:
  7.9 4.6 copy.74
  12.6 3.9 copy.75
  16.4 6.4 copy.76
  22.9 6.7 pad_maximum_fusion
  29.6 6.5 all-to-all-start
  38.6 174.2 %all_gather.17 = s32[1,1024]{1,0:T(1,128)S(1)} all-gather(s32[1,128]{1,0:T(1,128)S(1)} %copy-done.43), channel_id=1, replica_groups=mesh['dp'=4,'ctx'=8] {'ctx'}, dimensions={1}, use_global_device_ids=true | all-gather | bytes 4608 | tf_op jit(solution)/shard_map/all_gather | solution.py:98
  214.9 4.6 fusion.49
  219.5 29.4 %all-to-all-done = bf16[8,256,1792]{1,2,0:T(8,128)(2,1)} async-done(((bf16[8,256,1792]{1,2,0:T(8,128)(2,1)}), bf16[8,256,1792]{1,2,0:T(8,128)(2,1)}, u32[]{:S(2)}, u32[]{:S(2)}) %all-to-all-start) | async-done | bytes 7340064 | tf_op jit(solution)/shard_map/all_to_all | solution.py:86
  248.9 9.9 copy.77
  258.9 11.7 %fusion.22 = f32[1024,1792]{1,0:T(8,128)S(1)} fusion(bf16[2048,1792]{1,0:T(8,128)(2,1)} %bitcast.157, bf16[1,1024,2048]{2,1,0:T(8,128)(2,1)} %all-gather.5.cloned.1.call-done), kind=kOutput, calls=%fused_computation.37 | convolution fusion | flops 7516192768 | bytes 18874368 | tf_op jit(solution)/shard_map/dot_general | solution.py:43
  270.6 3.0 copy-done.5
  275.5 3.5 copy.78
  281.1 10.1 fusion.97
  291.3 9.6 fusion.39
  300.9 15.9 %multiply_reduce_fusion = (f32[4,1024]{1,0:T(4,128)S(1)}, f32[4,1024,1024]{1,2,0:T(8,128)}) fusion(f32[4,1024,1024]{1,2,0:T(8,128)} %get-tuple-element.112, f32[4,1024]{1,0:T(4,128)S(1)} %get-tuple-element.111, bf16[1024,4,64]{0,2,1:T(8,128)(2,1)} %bitcast.170, f32[1,1024,3,4,64]{1,4,3,2,0:T(8,128)} %bitcast.154), kind=kOutput, calls=%fused_computation.2 | convolution fusion | flops 549449728 | bytes 34635776 | tf_op jit(solution)/shard_map/sqhd,skhd->shqk/dot_general | solution.py:142
  316.8 8.1 multiply_convert_fusion
  324.9 2.7 fusion.42
  332.2 12.3 %convert_reduce_fusion = (f32[1024]{0:T(1024)}, bf16[1024,1024]{1,0:T(8,128)(2,1)S(1)}) fusion(f32[1024]{0:T(1024)S(1)} %copy-done.40, f32[1024,1792]{1,0:T(8,128)} %copy-done.5, bf16[1024,2048]{1,0:T(8,128)(2,1)} %param.24, bf16[1,1024,2048]{2,1,0:T(8,128)(2,1)} %all-gather.7.cloned.1.call-done), kind=kOutput, calls=%fused_computation.40 | convolution fusion | flops 4319083520 | bytes 14688256 | tf_op jit(solution)/shard_map/dot_general | solution.py:43
  344.5 8.7 convolution_convert_fusion
  353.2 7.0 copy.84
  360.3 12.0 %convert_bitcast_fusion.2 = bf16[1,1024,2048]{2,1,0:T(8,128)(2,1)} fusion(bf16[2048,1792]{1,0:T(8,128)(2,1)} %bitcast.158, bf16[1024,1024]{1,0:T(8,128)(2,1)} %copy-done.48, bf16[1024,768]{1,0:T(8,128)(2,1)S(1)} %copy-done.4), kind=kOutput, calls=%fused_computation.42 | convolution fusion | flops 7525629952 | bytes 15204352 | tf_op jit(solution)/shard_map/dot_general | solution.py:43
  373.3 9.1 fusion.46
  382.4 8.7 fusion.94
  391.1 3.3 fusion.30
  394.6 53.3 %reduce-scatter.8.cloned.1.call-done = bf16[8,64,1792]{2,0,1:T(8,128)(2,1)} async-done(((bf16[8,256,1792]{2,0,1:T(8,128)(2,1)}), bf16[8,64,1792]{2,0,1:T(8,128)(2,1)}) %reduce-scatter.8.cloned.1.call-update) | async-done | bytes 1835024 | tf_op jit(solution)/shard_map/reduce_scatter | solution.py:174
  447.9 3.0 copy.85
  450.9 4.6 all-to-all-start.1
  456.8 78.1 %reduce-scatter.6.cloned.1.call-done = bf16[1,128,2048]{2,1,0:T(8,128)(2,1)} async-done(((bf16[1,1024,2048]{2,1,0:T(8,128)(2,1)}), bf16[1,128,2048]{2,1,0:T(8,128)(2,1)}) %reduce-scatter.6.cloned.1.call-update) | async-done | bytes 524304 | tf_op jit(solution)/shard_map/reduce_scatter | solution.py:164
  537.0 53.4 %reduce-scatter.4.cloned.1.call-done = bf16[1,128,2048]{2,1,0:T(8,128)(2,1)} async-done(((bf16[1,1024,2048]{2,1,0:T(8,128)(2,1)}), bf16[1,128,2048]{2,1,0:T(8,128)(2,1)}) %reduce-scatter.4.cloned.1.call-update) | async-done | bytes 524304 | tf_op jit(solution)/shard_map/reduce_scatter | solution.py:129
  590.4 3.9 convert_reduce_fusion.4
  596.8 3.6 fusion.36
  600.4 8.4 convert_bitcast_fusion.1
  608.8 2.7 pad_maximum_fusion.1
  613.0 3.4 fusion.1
  616.5 38.1 %pmax.7 = f32[32]{0:T(128)S(1)} all-reduce(f32[32]{0:T(128)S(1)} %dynamic_update_slice.11), channel_id=1, replica_groups=mesh['dp'=4,'ctx'=8] {'dp','ctx'}, use_global_device_ids=true, to_apply=%region_22.23 | all-reduce | flops 32 | bytes 256 | tf_op jit(solution)/shard_map/pmax | solution.py:126
  655.4 4.1 convert_multiply_fusion
  659.5 58.9 %all-reduce.3.cloned.1.call-done = (f32[2048]{0:T(1024)}, f32[2048]{0:T(1024)}, f32[6144]{0:T(1024)}, f32[2048]{0:T(1024)}, f32[8192]{0:T(1024)}) async-done(((f32[2048]{0:T(1024)}, f32[2048]{0:T(1024)}, f32[6144]{0:T(1024)}, f32[2048]{0:T(1024)}, f32[8192]{0:T(1024)}), (f32[2048]{0:T(1024)}, f32[2048]{0:T(1024)}, f32[6144]{0:T(1024)}, f32[2048]{0:T(1024)}, f32[8192]{0:T(1024)})) %all-reduce.3.cloned.1.call-update) | async-done | bytes 81936 | tf_op jit(solution)/shard_map/psum | solution.py:206
  718.4 82.7 %all-gather.9.cloned.1.call-done = bf16[256,8,1792]{2,1,0:T(8,128)(2,1)} async-done(((bf16[64,8,1792]{2,1,0:T(8,128)(2,1)}), bf16[256,8,1792]{2,1,0:T(8,128)(2,1)}) %all-gather.9.cloned.1.call-update) | async-done | bytes 7340048 | tf_op jit(solution)/shard_map/all_gather | solution.py:178
  801.1 3.8 slice.136
  804.9 4.9 copy.94
  809.8 4.5 slice_convert_fusion.1
  814.2 11.0 %copy.96 = f32[32,8,8,1024]{3,1,2,0:T(8,128)} copy(f32[32,8,8,1024]{3,2,1,0:T(8,128)S(1)} %bitcast.145) | data formatting | bytes 16777216
  826.0 3.4 copy.88
  829.3 6.8 copy.89
  836.2 160.0 %all-gather.11.cloned.1.call-done = bf16[4,1280,2048]{2,1,0:T(8,128)(2,1)} async-done(((bf16[1,1280,2048]{2,1,0:T(8,128)(2,1)}), bf16[4,1280,2048]{2,1,0:T(8,128)(2,1)}) %all-gather.11.cloned.1.call-update) | async-done | bytes 20971536 | tf_op jit(solution)/shard_map/all_gather | solution.py:188
  996.2 14.8 %reduce_sum.120 = bf16[1280,2048]{1,0:T(8,128)(2,1)} reduce(bf16[4,1280,2048]{2,1,0:T(8,128)(2,1)} %all-gather.11.cloned.1.call-done, bf16[]{:T(256)} %constant.54.clone.1), dimensions={0}, to_apply=%region_16.17 | reduce | flops 7864320 | bytes 26214402 | tf_op jit(solution)/shard_map/reduce_sum | solution.py:187
  1011.1 2.8 slice_convert_fusion.2
  1013.9 6.7 slice_convert_fusion
  (178 shorter events, 27.4 us)
Async XLA Ops:
  7.2 207.7 %copy-start = (bf16[256,2048]{1,0:T(8,128)(2,1)S(1)}, bf16[256,2048]{1,0:T(8,128)(2,1)}, u32[]{:S(2)}) copy-start(bf16[256,2048]{1,0:T(8,128)(2,1)} %param.20) | copy-start | bytes 3145732
  7.2 207.7 %all-gather.7.cloned.1.call-start = ((), (), s32[]{:S(2)}) async-start(), calls=%async_computation.7 | async-start | bytes 4718592 | tf_op jit(solution)/shard_map/all_gather | solution.py:89
  29.6 6.6 copy-start.1
  29.6 7.8 copy-start.24
  29.6 7.8 copy-start.33
  29.6 9.1 copy-start.43
  29.6 183.3 %copy-start.26 = (f32[6144]{0:T(1024)S(1)}, f32[6144]{0:T(1024)}, u32[]{:S(2)}) copy-start(f32[6144]{0:T(1024)} %param.19) | copy-start | bytes 73732
  29.6 219.4 %all-to-all-start = ((bf16[8,256,1792]{1,2,0:T(8,128)(2,1)}), bf16[8,256,1792]{1,2,0:T(8,128)(2,1)}, u32[]{:S(2)}, u32[]{:S(2)}) async-start(bf16[8,256,1792]{1,2,0:T(8,128)(2,1)} %pad_maximum_fusion), calls=%async_computation | async-start | bytes 14680064 | tf_op jit(solution)/shard_map/all_to_all | solution.py:86
  36.1 222.8 %all-gather.5.cloned.1.call-start = ((), (), s32[]{:S(2)}) async-start(), calls=%async_computation.5 | async-start | bytes 4718592 | tf_op jit(solution)/shard_map/all_gather | solution.py:95
  38.6 409.3 %reduce-scatter.8.cloned.1.call-start = ((), (), s32[]{:S(2)}) async-start(), calls=%async_computation.9 | async-start | bytes 9175040 | tf_op jit(solution)/shard_map/reduce_scatter | solution.py:174
  214.9 76.4 %copy-start.6 = (pred[1024,1024]{0,1:T(8,128)(4,1)}, pred[1024,1024]{0,1:T(8,128)(4,1)S(1)}, u32[]{:S(2)}) copy-start(pred[1024,1024]{0,1:T(8,128)(4,1)S(1)} %iota_compare_fusion) | copy-start | bytes 3145732
  280.7 10.5 %copy-start.10 = (bf16[1024,4,32]{0,2,1:T(8,128)(2,1)}, bf16[1024,4,32]{0,2,1:T(8,128)(2,1)S(1)}, u32[]{:S(2)}) copy-start(bf16[1024,4,32]{0,2,1:T(8,128)(2,1)S(1)} %get-tuple-element.118) | copy-start | bytes 786436
  280.8 91.8 %copy-start.8 = (bf16[1024,4,32]{0,2,1:T(8,128)(2,1)}, bf16[1024,4,32]{0,2,1:T(8,128)(2,1)S(1)}, u32[]{:S(2)}) copy-start(bf16[1024,4,32]{0,2,1:T(8,128)(2,1)S(1)} %get-tuple-element.117) | copy-start | bytes 786436
  281.1 10.1 copy-start.13
  281.1 10.1 copy-start.16
  300.8 15.9 %slice-start = ((s8[16777216]{0:T(1024)(128)(4,1)}), s8[4194304]{0:T(1024)(128)(4,1)S(1)}, s32[]{:S(2)}) async-start(s8[16777216]{0:T(1024)(128)(4,1)} %bitcast.148), calls=%async_computation.13 | async-start | bytes 8388608
  300.8 15.9 %slice-start.1 = ((s8[16777216]{0:T(1024)(128)(4,1)}), s8[4194304]{0:T(1024)(128)(4,1)S(1)}, s32[]{:S(2)}) async-start(s8[16777216]{0:T(1024)(128)(4,1)} %bitcast.148), calls=%async_computation.14 | async-start | bytes 8388608
  300.8 15.9 %slice-start.2 = ((s8[16777216]{0:T(1024)(128)(4,1)}), s8[4194304]{0:T(1024)(128)(4,1)S(1)}, s32[]{:S(2)}) async-start(s8[16777216]{0:T(1024)(128)(4,1)} %bitcast.148), calls=%async_computation.15 | async-start | bytes 8388608
  300.9 15.9 %slice-start.3 = ((s8[16777216]{0:T(1024)(128)(4,1)}), s8[4194304]{0:T(1024)(128)(4,1)S(1)}, s32[]{:S(2)}) async-start(s8[16777216]{0:T(1024)(128)(4,1)} %bitcast.148), calls=%async_computation.16 | async-start | bytes 8388608
  316.8 8.1 copy-start.14
  332.2 12.3 %copy-start.4 = (bf16[1024,768]{1,0:T(8,128)(2,1)S(1)}, bf16[1024,768]{1,0:T(8,128)(2,1)}, u32[]{:S(2)}) copy-start(bf16[1024,768]{1,0:T(8,128)(2,1)} %copy.83) | copy-start | bytes 4718596
  332.2 12.3 %copy-start.45 = (bf16[1,1024,2048]{2,1,0:T(8,128)(2,1)S(1)}, bf16[1,1024,2048]{2,1,0:T(8,128)(2,1)}, u32[]{:S(2)}) copy-start(bf16[1,1024,2048]{2,1,0:T(8,128)(2,1)} %all-gather.5.cloned.1.call-done) | copy-start | bytes 12582916
  344.5 8.7 copy-start.48
  360.2 174.6 %reduce-scatter.6.cloned.1.call-start = ((), (), s32[]{:S(2)}) async-start(), calls=%async_computation.8 | async-start | bytes 4718592 | tf_op jit(solution)/shard_map/reduce_scatter | solution.py:164
  372.3 218.1 %reduce-scatter.4.cloned.1.call-start = ((), (), s32[]{:S(2)}) async-start(), calls=%async_computation.6 | async-start | bytes 4718592 | tf_op jit(solution)/shard_map/reduce_scatter | solution.py:129
  382.4 8.7 copy-start.20
  394.5 62.0 %copy-start.42 = (f32[1024]{0:T(1024)S(1)}, f32[1024]{0:T(1024)}, u32[]{:S(2)}) copy-start(f32[1024]{0:T(1024)} %get-tuple-element.115) | copy-start | bytes 12292
  394.5 140.4 %copy-start.2 = (bf16[1,128,2048]{2,1,0:T(8,128)(2,1)S(1)}, bf16[1,128,2048]{2,1,0:T(8,128)(2,1)}, u32[]{:S(2)}) copy-start(bf16[1,128,2048]{2,1,0:T(8,128)(2,1)} %param.14) | copy-start | bytes 1572868
  394.5 140.4 %copy-start.25 = (f32[2048]{0:T(1024)S(1)}, f32[2048]{0:T(1024)}, u32[]{:S(2)}) copy-start(f32[2048]{0:T(1024)} %param.16) | copy-start | bytes 24580
  394.5 140.3 %copy-start.32 = (f32[128]{0:T(128)S(1)}, f32[128]{0:T(128)}, u32[]{:S(2)}) copy-start(f32[128]{0:T(128)} %copy-done.31) | copy-start | bytes 1540
  394.5 140.3 %copy-start.39 = (f32[128]{0:T(128)S(1)}, f32[128]{0:T(128)}, u32[]{:S(2)}) copy-start(f32[128]{0:T(128)} %copy-done.38) | copy-start | bytes 1540
  394.6 195.9 %copy-start.34 = (f32[2048]{0:T(1024)S(1)}, f32[2048]{0:T(1024)}, u32[]{:S(2)}) copy-start(f32[2048]{0:T(1024)} %param.25) | copy-start | bytes 24580
  394.6 195.9 %copy-start.35 = (f32[2048]{0:T(1024)S(1)}, f32[2048]{0:T(1024)}, u32[]{:S(2)}) copy-start(f32[2048]{0:T(1024)} %param.21) | copy-start | bytes 24580
  450.9 143.5 %all-to-all-start.1 = ((bf16[8,64,1792]{2,1,0:T(8,128)(2,1)}), bf16[8,64,1792]{2,1,0:T(8,128)(2,1)S(1)}, u32[]{:S(2)}, u32[]{:S(2)}) async-start(bf16[8,64,1792]{2,1,0:T(8,128)(2,1)} %copy.85), calls=%async_computation.4 | async-start | bytes 3670016 | tf_op jit(solution)/shard_map/all_to_all | solution.py:177
  455.5 262.9 %all-reduce.3.cloned.1.call-start = ((), (), s32[]{:S(2)}) async-start(), calls=%async_computation.12 | async-start | bytes 163840 | tf_op jit(solution)/shard_map/psum | solution.py:206
  456.8 137.6 %copy-start.23 = (f32[8192]{0:T(1024)}, f32[8192]{0:T(1024)S(1)}, u32[]{:S(2)}) copy-start(f32[8192]{0:T(1024)S(1)} %dynamic_update_slice.10) | copy-start | bytes 98308
  594.4 206.8 %all-gather.9.cloned.1.call-start = ((), (), s32[]{:S(2)}) async-start(), calls=%async_computation.10 | async-start | bytes 9175040 | tf_op jit(solution)/shard_map/all_gather | solution.py:178
  596.7 3.7 copy-start.41
  596.7 399.5 %all-gather.11.cloned.1.call-start = ((), (), s32[]{:S(2)}) async-start(), calls=%async_computation.11 | async-start | bytes 26214400 | tf_op jit(solution)/shard_map/all_gather | solution.py:188
  613.0 41.6 %copy-start.46 = (s32[32]{0:T(128)S(1)}, s32[32]{0:T(128)}, u32[]{:S(2)}) copy-start(s32[32]{0:T(128)} %param.26) | copy-start | bytes 388
  613.0 41.8 %copy-start.27 = (f32[6144]{0:T(1024)S(1)}, f32[6144]{0:T(1024)}, u32[]{:S(2)}) copy-start(f32[6144]{0:T(1024)} %param.19) | copy-start | bytes 73732
  654.6 150.3 %copy-start.47 = (f32[32]{0:T(128)}, f32[32]{0:T(128)S(1)}, u32[]{:S(2)}) copy-start(f32[32]{0:T(128)S(1)} %pmax.7) | copy-start | bytes 388
  814.2 11.0 %copy-start.3 = (bf16[256,8,768]{0,2,1:T(8,128)(2,1)S(1)}, bf16[256,8,768]{0,2,1:T(8,128)(2,1)}, u32[]{:S(2)}) copy-start(bf16[256,8,768]{0,2,1:T(8,128)(2,1)} %copy.94) | copy-start | bytes 9437188
  1013.9 6.7 copy-start.29
  1013.9 7.3 copy-start.37
  1013.9 7.9 copy-start.36
  1013.9 8.5 copy-start.30
  1013.9 9.7 copy-start.28
  (15 other events, 26.7 us)
Sparse Core Ops, SparseCore 0:
  9.6 67.6 all-gather.6
  79.5 135.0 all-gather.4
  360.4 87.4 reduce-scatter.7
  450.6 84.2 reduce-scatter.5
  537.6 52.8 reduce-scatter.3
  597.9 120.5 all-reduce.2
  720.9 80.2 all-gather.8
  803.0 193.1 all-gather.10
